TPU v7x, 32 devices: a whole 2x2x4 slice. The times are simulated.
32 devices in a mesh: layer: 4 (over x, core), ex: 8 (over z, y).
Axes of the slice: x: 2, y: 2, z: 4, core: 2. Of those that a mesh axis runs over, the one named last changes fastest.
Arguments:
- queries: bfloat16 [128, 8, 4096], P('ex', 'layer'), may hold values from -6 to 6
- stored: bfloat16 [2048, 8, 4096], P('ex', 'layer'), may hold values from -0.03125 to 0.03125
- left_inv: bfloat16 [8, 64, 64], P('layer'), may hold values from -0.078125 to 2
- right_inv: bfloat16 [8, 64, 64], P('layer'), may hold values from -0.078125 to 2
Outputs:
- scores: float32 [128, 2048], P('layer', 'ex')
All inputs are finite; a program needn't handle non-finite values.
Results may differ from a plain program's by a relative error of at most 0.0041.
Values may be sent and summed in bfloat16 or wider, within the bound.
A program may use at most 128 MiB of HBM per device.

v0:
```python
import jax
import jax.numpy as jnp
from jax import lax
from jax.sharding import PartitionSpec as P


def precondition(gradients, left_inv, right_inv):
    count = gradients.shape[0]
    layers_here = gradients.shape[1]
    side = left_inv.shape[1]
    mats = gradients.reshape(count, layers_here, side, side)
    left_side = jnp.einsum(
        "lia,qlaj->qlij", left_inv, mats, preferred_element_type=jnp.float32
    ).astype(jnp.bfloat16)
    ready = jnp.einsum(
        "qlib,lbj->qlij", left_side, right_inv, preferred_element_type=jnp.float32
    ).astype(jnp.bfloat16)
    return ready.reshape(count, layers_here * side * side)


def shards(queries, stored, left_inv, right_inv):
    stored_flat = stored.reshape(stored.shape[0], stored.shape[1] * stored.shape[2])
    own_ready = precondition(queries, left_inv, right_inv)
    partial_value = lax.dot_general(
        lax.all_gather(own_ready, "ex", axis=0, tiled=True),
        stored_flat,
        (((1,), (1,)), ((), ())),
        preferred_element_type=jnp.float32,
    )
    return lax.psum_scatter(partial_value, "layer", scatter_dimension=0, tiled=True)


def solution(mesh):
    placed = (
        P("ex", "layer", None),
        P("ex", "layer", None),
        P("layer", None, None),
        P("layer", None, None),
    )
    return jax.shard_map(
        shards, mesh=mesh, in_specs=placed, out_specs=P("layer", "ex"), check_vma=False
    )
```

profile of v0, /device:TPU:0, one launch (start us, length us, event | category | flops | bytes accessed | tf_op | source)
XLA Modules:
  0.0 92.5 jit_solution(12882949968957154672)
XLA Ops:
  6.5 0.0 copy-start
  6.5 0.0 all-gather.2.cloned.1.call-start
  6.5 1.3 %reshape.9 = bf16[16,2,64,64]{3,2,1,0:T(8,128)(2,1)S(1)} reshape(bf16[16,2,4096]{2,1,0:T(2,128)(2,1)} %param.4) | data formatting | bytes 524288 | tf_op jit(solution)/shard_map/reshape | solution.py:11
  7.9 0.0 copy-done
  7.9 1.2 %fusion = bf16[16,2,64,64]{3,2,0,1:T(8,128)(2,1)S(1)} fusion(bf16[16,2,64,64]{3,2,1,0:T(8,128)(2,1)S(1)} %reshape.9, bf16[2,64,64]{2,1,0:T(8,128)(2,1)S(1)} %copy-done, bf16[2,64,64]{2,1,0:T(8,128)(2,1)} %param.6), kind=kOutput, calls=%fused_computation.2 | convolution fusion | flops 33816576 | bytes 557056 | tf_op jit(solution)/shard_map/qlib,lbj->qlij/dot_general | solution.py:15
  9.2 1.2 %reshape.10 = bf16[16,8192]{1,0:T(8,128)(2,1)} reshape(bf16[16,2,64,64]{3,2,1,0:T(8,128)(2,1)S(1)} %copy.5) | data formatting | bytes 524288 | tf_op jit(solution)/shard_map/reshape | solution.py:18
  10.3 0.0 all-gather.2.cloned.1.call-update
  10.4 0.0 reduce-scatter.2.cloned.1.call-start
  10.4 8.6 %copy.9 = bf16[32,8,2,4096]{3,1,2,0:T(8,128)(2,1)} copy(bf16[32,8,2,4096]{3,2,1,0:T(2,128)(2,1)} %bitcast.24) | data formatting | bytes 8388608
  19.0 43.3 %all-gather.2.cloned.1.call-done = bf16[128,8192]{1,0:T(8,128)(2,1)} async-done(((bf16[16,8192]{1,0:T(8,128)(2,1)}), bf16[128,8192]{1,0:T(8,128)(2,1)}) %all-gather.2.cloned.1.call-update) | async-done | bytes 2097168 | tf_op jit(solution)/shard_map/all_gather | solution.py:25
  62.3 5.0 %fusion.7 = f32[128,256]{1,0:T(8,128)} fusion(bf16[128,8192]{1,0:T(8,128)(2,1)} %all-gather.2.cloned.1.call-done, bf16[256,8192]{1,0:T(8,128)(2,1)} %bitcast.23), kind=kOutput, calls=%fused_computation.7 | convolution fusion | flops 536870912 | bytes 6422528 | tf_op jit(solution)/shard_map/dot_general | solution.py:24
  67.3 0.0 reduce-scatter.2.cloned.1.call-update
  67.4 18.3 %reduce-scatter.2.cloned.1.call-done = f32[32,256]{1,0:T(8,128)} async-done(((f32[128,256]{1,0:T(8,128)}), f32[32,256]{1,0:T(8,128)}) %reduce-scatter.2.cloned.1.call-update) | async-done | bytes 32784 | tf_op jit(solution)/shard_map/reduce_scatter | solution.py:30
  (1 shorter events, 0.0 us)
Async XLA Ops:
  6.5 1.4 %copy-start = (bf16[2,64,64]{2,1,0:T(8,128)(2,1)S(1)}, bf16[2,64,64]{2,1,0:T(8,128)(2,1)}, u32[]{:S(2)}) copy-start(bf16[2,64,64]{2,1,0:T(8,128)(2,1)} %param.7) | copy-start | bytes 49156
  6.5 55.8 %all-gather.2.cloned.1.call-start = ((), (), s32[]{:S(2)}) async-start(), calls=%async_computation.1 | async-start | bytes 2359296 | tf_op jit(solution)/shard_map/all_gather | solution.py:25
  10.4 75.3 %reduce-scatter.2.cloned.1.call-start = ((), (), s32[]{:S(2)}) async-start(), calls=%async_computation.2 | async-start | bytes 163840 | tf_op jit(solution)/shard_map/reduce_scatter | solution.py:30
Sparse Core Ops, SparseCore 0:
  10.5 51.7 all-gather.1
  67.5 18.1 reduce-scatter.1
where the time goes:
time: 92.8 us; the launch traced here: 92.5 us
  waiting for transfers between devices  61.6 us (66%)
  between operations  13.4 us (14%)
  local copies, waits for them, and re-layouts  11.2 us (12%)
  matrix products  6.23 us (7%)
    all_gather x1, waiting for transfers between devices, shards(): lax.all_gather(own_ready, 'ex', axis=0, tiled=True)  43.3 us
    reduce_scatter x1, waiting for transfers between devices, shards(): lax.psum_scatter(partial_value, 'layer', scatter_dimension=0, tiled=True)  18.3 us
    unnamed x3, local copies, waits for them, and re-layouts  8.62 us
    dot_general x1, matrix products, shards(): lax.dot_general(lax.all_gather(own_ready, 'ex', axis=0, tiled=True), stor...  5.01 us
  transfers between devices with their start and end apart: 2, of which 2 were waited for; matrix products, arithmetic and copies ran while one was open for 9% of the time, Pallas kernels for 0%

commit v1 on v0

--- a/solution.py
+++ b/solution.py
@@ -2,6 +2,14 @@
 import jax.numpy as jnp
 from jax import lax
 from jax.sharding import PartitionSpec as P
+
+
+def handle_members_all_up(net_axis, m):
+    n_slots = lax.axis_size(net_axis)
+    vals = tuple((n_slots if rr == 0 else 1 for rr in range(m.ndim)))
+    heard = jnp.tile(m, vals)
+    moved = lax.all_to_all(heard, net_axis, tiled=True, split_axis=0, concat_axis=0)
+    return moved
 
 
 def precondition(gradients, left_inv, right_inv):
@@ -22,7 +30,7 @@
     stored_flat = stored.reshape(stored.shape[0], stored.shape[1] * stored.shape[2])
     own_ready = precondition(queries, left_inv, right_inv)
     partial_value = lax.dot_general(
-        lax.all_gather(own_ready, "ex", axis=0, tiled=True),
+        handle_members_all_up("ex", own_ready),
         stored_flat,
         (((1,), (1,)), ((), ())),
         preferred_element_type=jnp.float32,

time: 92.8 us -> 97.1 us (1.046)
  starting transfers between devices: 0.04 us -> 7.35 us
  waiting for transfers between devices: 61.6 us -> 58.4 us
    all_gather x1 -> x0, waiting for transfers between devices: 43.3 us -> none  [shards(): lax.all_gather(own_ready, 'ex', axis=0, tiled=True)]
    all_to_all x0 -> x1, waiting for transfers between devices: none -> 39.6 us  [handle_members_all_up(): lax.all_to_all(heard, net_axis, tiled=True, split_axis=0, concat_axis=0)]
    all_to_all x0 -> x1, starting transfers between devices: none -> 7.31 us  [handle_members_all_up(): lax.all_to_all(heard, net_axis, tiled=True, split_axis=0, concat_axis=0)]
    another operation x0 -> x2, local copies, waits for them, and re-layouts: none -> 1.98 us  [handle_members_all_up(): heard = jnp.tile(m, vals)]
    reshape x1 -> x0, local copies, waits for them, and re-layouts: 1.18 us -> none  [precondition(): return ready.reshape(count, layers_here * side * side)]
where the time goes in v1:
time: 97.1 us; the launch traced here: 96.8 us
  waiting for transfers between devices  58.4 us (60%)
  between operations  13.4 us (14%)
  local copies, waits for them, and re-layouts  12 us (12%)
  starting transfers between devices  7.35 us (8%)
  matrix products  5.59 us (6%)
    all_to_all x1, waiting for transfers between devices, handle_members_all_up(): lax.all_to_all(heard, net_axis, tiled=True, split_axis=0, concat_axis=0)  39.6 us
    reduce_scatter x1, waiting for transfers between devices, shards(): lax.psum_scatter(partial_value, 'layer', scatter_dimension=0, tiled=True)  18.9 us
    unnamed x3, local copies, waits for them, and re-layouts  8.62 us
    all_to_all x1, starting transfers between devices, handle_members_all_up(): lax.all_to_all(heard, net_axis, tiled=True, split_axis=0, concat_axis=0)  7.31 us
    dot_general x1, matrix products, shards(): lax.dot_general(handle_members_all_up('ex', own_ready), stored_flat, (((1...  4.37 us
    another operation x2, local copies, waits for them, and re-layouts, handle_members_all_up(): heard = jnp.tile(m, vals)  1.98 us
  transfers between devices with their start and end apart: 2, of which 2 were waited for; matrix products, arithmetic and copies ran while one was open for 9% of the time, Pallas kernels for 0%

profile of v1, /device:TPU:0, one launch (start us, length us, event | category | flops | bytes accessed | tf_op | source)
XLA Modules:
  0.0 96.8 jit_solution(8803114477664471187)
XLA Ops:
  6.5 0.0 copy-start
  6.5 1.3 %reshape.13 = bf16[16,2,64,64]{3,2,1,0:T(8,128)(2,1)S(1)} reshape(bf16[16,2,4096]{2,1,0:T(2,128)(2,1)} %param.4) | data formatting | bytes 524288 | tf_op jit(solution)/shard_map/reshape | solution.py:19
  7.9 0.0 copy-done
  7.9 1.2 %fusion = bf16[16,2,64,64]{3,2,0,1:T(8,128)(2,1)S(1)} fusion(bf16[16,2,64,64]{3,2,1,0:T(8,128)(2,1)S(1)} %reshape.13, bf16[2,64,64]{2,1,0:T(8,128)(2,1)S(1)} %copy-done, bf16[2,64,64]{2,1,0:T(8,128)(2,1)} %param.6), kind=kOutput, calls=%fused_computation.2 | convolution fusion | flops 33816576 | bytes 557056 | tf_op jit(solution)/shard_map/qlib,lbj->qlij/dot_general | solution.py:23
  9.2 0.5 tile.8
  9.6 1.5 %tile.9 = bf16[8,16,8192]{2,1,0:T(8,128)(2,1)} broadcast(bf16[16,8192]{1,0:T(8,128)(2,1)S(1)} %tile.8), dimensions={1,2} | broadcast | bytes 2359296 | tf_op jit(solution)/shard_map/tile | solution.py:10
  11.1 7.3 %all-to-all-start = ((bf16[8,16,8192]{2,1,0:T(8,128)(2,1)}), bf16[8,16,8192]{2,1,0:T(8,128)(2,1)S(1)}, u32[]{:S(2)}, u32[]{:S(2)}) async-start(bf16[8,16,8192]{2,1,0:T(8,128)(2,1)} %tile.9), calls=%async_computation | async-start | bytes 4194304 | tf_op jit(solution)/shard_map/all_to_all | solution.py:11
  18.5 0.0 reduce-scatter.2.cloned.1.call-start
  18.5 8.6 %copy.9 = bf16[32,8,2,4096]{3,1,2,0:T(8,128)(2,1)} copy(bf16[32,8,2,4096]{3,2,1,0:T(2,128)(2,1)} %bitcast.26) | data formatting | bytes 8388608
  27.1 39.6 %all-to-all-done = bf16[8,16,8192]{2,1,0:T(8,128)(2,1)S(1)} async-done(((bf16[8,16,8192]{2,1,0:T(8,128)(2,1)}), bf16[8,16,8192]{2,1,0:T(8,128)(2,1)S(1)}, u32[]{:S(2)}, u32[]{:S(2)}) %all-to-all-start) | async-done | bytes 2097184 | tf_op jit(solution)/shard_map/all_to_all | solution.py:11
  66.7 4.4 %fusion.7 = f32[128,256]{1,0:T(8,128)} fusion(bf16[128,8192]{1,0:T(8,128)(2,1)S(1)} %bitcast.25, bf16[256,8192]{1,0:T(8,128)(2,1)} %bitcast.24), kind=kOutput, calls=%fused_computation.7 | convolution fusion | flops 536870912 | bytes 6422528 | tf_op jit(solution)/shard_map/dot_general | solution.py:32
  71.1 0.0 reduce-scatter.2.cloned.1.call-update
  71.1 18.9 %reduce-scatter.2.cloned.1.call-done = f32[32,256]{1,0:T(8,128)} async-done(((f32[128,256]{1,0:T(8,128)}), f32[32,256]{1,0:T(8,128)}) %reduce-scatter.2.cloned.1.call-update) | async-done | bytes 32784 | tf_op jit(solution)/shard_map/reduce_scatter | solution.py:38
  (1 shorter events, 0.0 us)
Async XLA Ops:
  6.5 1.3 %copy-start = (bf16[2,64,64]{2,1,0:T(8,128)(2,1)S(1)}, bf16[2,64,64]{2,1,0:T(8,128)(2,1)}, u32[]{:S(2)}) copy-start(bf16[2,64,64]{2,1,0:T(8,128)(2,1)} %param.7) | copy-start | bytes 49156
  11.1 55.5 %all-to-all-start = ((bf16[8,16,8192]{2,1,0:T(8,128)(2,1)}), bf16[8,16,8192]{2,1,0:T(8,128)(2,1)S(1)}, u32[]{:S(2)}, u32[]{:S(2)}) async-start(bf16[8,16,8192]{2,1,0:T(8,128)(2,1)} %tile.9), calls=%async_computation | async-start | bytes 4194304 | tf_op jit(solution)/shard_map/all_to_all | solution.py:11
  18.5 71.5 %reduce-scatter.2.cloned.1.call-start = ((), (), s32[]{:S(2)}) async-start(), calls=%async_computation.2 | async-start | bytes 163840 | tf_op jit(solution)/shard_map/reduce_scatter | solution.py:38
Sparse Core Ops, SparseCore 0:
  71.2 18.6 reduce-scatter.1
